TPU v7x, 32 devices: a whole 2x2x4 slice. The times are simulated.
32 devices in a mesh: clip: 8 (over y, x, core), tm: 4 (over z).
Axes of the slice: x: 2, y: 2, z: 4, core: 2. Of those that a mesh axis runs over, the one named last changes fastest.
Arguments:
- latent: bfloat16 [8, 32, 8, 32, 16], P('clip', 'tm'), may hold values from -6 to 6
- offsets: int32 [8], P('clip'), may hold values from 0 to 16
- teacher: bfloat16 [8, 32, 8, 16, 384], P('clip', 'tm'), may hold values from -6 to 6
- w_in: bfloat16 [432, 384], replicated, may hold values from -0.3125 to 0.3125
- w_mid: bfloat16 [10368, 384], P('clip'), may hold values from -0.0625 to 0.0625
Outputs:
- grad_mid: float32 [10368, 384], P('clip')
- grad_in: float32 [432, 384], replicated
Inputs may be any that keep to these rules, and one draw needn't show every extreme that they name: `offsets`: each clip's crop start among the latent columns.
All inputs are finite; a program needn't handle non-finite values.
Results may differ from a plain program's by a relative error of at most 0.00095.
Values may be sent and summed in bfloat16 or wider, within the bound.
No kernel may reach another device: no remote copies, remote signals or barrier semaphores. Data moves between devices by JAX's collectives and lax.ppermute only.
A program may use at most 192 MiB of HBM per device.

v0:
```python
import math
import jax
import jax.numpy as jnp
from jax import lax
from jax.sharding import PartitionSpec as P


def passed_along(block, axis, distance):
    devices = range(lax.axis_size(axis))
    route = [(i - distance, i) for i in devices if i - distance in devices]
    return lax.ppermute(block, axis, route)


def tap_masks(count, rows, cols):
    place = jnp.arange(count, dtype=jnp.int32) % (rows * cols)
    row_pos = place // cols
    col_pos = place % cols
    masks = []
    for row_off in range(3):
        for col_off in range(3):
            good_row = (row_pos + row_off - 1 >= 0) & (row_pos + row_off - 1 < rows)
            good_col = (col_pos + col_off - 1 >= 0) & (col_pos + col_off - 1 < cols)
            masks.append((good_row & good_col).astype(jnp.bfloat16).reshape(count, 1))
    return masks


def tap_slices(extended, count, rows, cols, masks):
    margin = jnp.zeros((cols + 1, extended.shape[1]), extended.dtype)
    padded = jnp.concatenate([margin, extended, margin], axis=0)
    plane = rows * cols
    pieces = []
    for depth in range(3):
        for row_off in range(3):
            for col_off in range(3):
                first = depth * plane + row_off * cols + col_off
                pieces.append(padded[first : first + count] * masks[row_off * 3 + col_off])
    return pieces


def cross_dot(left, right):
    return lax.dot_general(
        left, right, (((0,), (0,)), ((), ())), preferred_element_type=jnp.float32
    )


def shards(latent, offsets, teacher, w_in, w_mid):
    frames = teacher.shape[1]
    rows = teacher.shape[2]
    cols = teacher.shape[3]
    chans = teacher.shape[4]
    plane = rows * cols
    count = frames * plane
    lat_chans = latent.shape[4]
    total_cells = lax.axis_size("clip") * lax.axis_size("tm") * count
    scale = 2.0 / math.sqrt(total_cells)
    masks = tap_masks(count, rows, cols)
    crop = lax.dynamic_slice_in_dim(latent[0], offsets[0], cols, axis=2).reshape(count, lat_chans)
    earlier = passed_along(crop[count - 2 * plane :], "tm", 1)
    crop_ext = jnp.concatenate([earlier, crop], axis=0)
    patch_in = jnp.concatenate(tap_slices(crop_ext, count, rows, cols, masks), axis=1)
    z_first = jnp.dot(patch_in, w_in, preferred_element_type=jnp.float32)
    act = jax.nn.silu(z_first).astype(jnp.bfloat16)
    act_prev = passed_along(act[count - 2 * plane :], "tm", 1)
    act_ext = jnp.concatenate([act_prev, act], axis=0)
    act_taps = tap_slices(act_ext, count, rows, cols, masks)
    w_full = lax.all_gather(w_mid, "clip", axis=0, tiled=True)
    output = jnp.zeros((count, chans), jnp.float32)
    for k in range(27):
        output = output + jnp.dot(
            act_taps[k], w_full[k * chans : (k + 1) * chans], preferred_element_type=jnp.float32
        )
    target_rows = teacher[0].reshape(count, chans).astype(jnp.float32)
    grad_low = ((output - target_rows) * scale).astype(jnp.bfloat16)
    local_mid = jnp.concatenate([cross_dot(act_taps[k], grad_low) for k in range(27)], axis=0)
    lead = 2 * plane + cols + 1
    masked_pads = []
    for k in range(9):
        masked_pads.append(jnp.pad(grad_low * masks[k], ((lead, lead), (0, 0))))
    ext_count = count + 2 * plane
    adjoint = jnp.zeros((ext_count, chans), jnp.float32)
    for depth in range(3):
        for row_off in range(3):
            for col_off in range(3):
                k = depth * 9 + row_off * 3 + col_off
                first = (2 - depth) * plane + (2 - row_off) * cols + (2 - col_off)
                piece = masked_pads[row_off * 3 + col_off][first : first + ext_count]
                adjoint = adjoint + lax.dot_general(
                    piece,
                    w_full[k * chans : (k + 1) * chans],
                    (((1,), (1,)), ((), ())),
                    preferred_element_type=jnp.float32,
                )
    outgoing = adjoint[: 2 * plane]
    incoming = passed_along(outgoing.astype(jnp.bfloat16), "tm", -1).astype(outgoing.dtype)
    own = adjoint[2 * plane :]
    dact = jnp.concatenate([own[: count - 2 * plane], own[count - 2 * plane :] + incoming], axis=0)
    sig = jax.nn.sigmoid(z_first)
    dz_first = (dact * sig * (1.0 + z_first * (1.0 - sig))).astype(jnp.bfloat16)
    grad_in = lax.psum(cross_dot(patch_in, dz_first), ("clip", "tm"))
    summed = lax.psum(local_mid, "tm")
    grad_mid = lax.psum_scatter(summed, "clip", scatter_dimension=0, tiled=True)
    return (grad_mid, grad_in)


def solution(mesh):
    return jax.shard_map(
        shards,
        mesh=mesh,
        in_specs=(
            P("clip", "tm", None, None, None),
            P("clip"),
            P("clip", "tm", None, None, None),
            P(),
            P("clip", None),
        ),
        out_specs=(P("clip", None), P()),
        check_vma=False,
    )
```

profile of v0, /device:TPU:0, one launch (start us, length us, event | category | flops | bytes accessed | tf_op | source)
XLA Modules:
  0.0 524.9 jit_solution(12850490637867089896)
XLA Ops:
  9.7 4.9 collective-permute-start
  18.5 2.0 multiply_convert_fusion
  20.5 3.9 collective-permute-start.1
  24.4 3.4 collective-permute-done.1
  27.8 2.3 concatenate.47
  30.2 35.1 %all-gather.2.cloned.1.call-done = bf16[10368,384]{1,0:T(8,128)(2,1)} async-done(((bf16[1296,384]{1,0:T(8,128)(2,1)}), bf16[10368,384]{1,0:T(8,128)(2,1)}) %all-gather.2.cloned.1.call-update) | async-done | bytes 7962640 | tf_op jit(solution)/shard_map/all_gather | solution.py:66
  65.3 3.0 fusion.52
  68.3 2.8 fusion.51
  71.1 2.8 fusion.50
  81.4 1.9 fusion.123
  90.7 1.9 fusion.108
  96.4 2.0 fusion.99
  100.2 2.1 fusion.93
  106.1 1.9 fusion.84
  111.8 1.9 fusion.48
  113.7 1.9 fusion.45
  117.4 17.8 %broadcast_multiply_fusion = (bf16[1024,384]{1,0:T(8,128)(2,1)S(1)}, bf16[1024,384]{1,0:T(8,128)(2,1)S(1)}, bf16[1024,384]{1,0:T(8,128)(2,1)S(1)}, bf16[1024,384...) fusion(bf16[1024]{0:T(1024)(128)(2,1)S(1)} %get-tuple-element.1, ...), kind=kOutput, calls=%fused_computation.165 | convolution fusion | flops 319684608 | bytes 50843648 | tf_op jit(solution)/shard_map/dot_general | solution.py:69
  135.3 3.1 convolution_dynamic-update-slice_fusion.26
  181.4 2.0 fusion.4
  210.1 7.5 %collective-permute-done.2 = bf16[256,384]{1,0:T(8,128)(2,1)S(1)} collective-permute-done((bf16[256,384]{1,0:T(8,128)(2,1)S(1)}, bf16[256,384]{1,0:T(8,128)(2,1)S(1)}, u32[]{:S(2)}, u32[]{:S(2)}) %collective-permute-start.2) | collective-permute-done | bytes 196640 | tf_op jit(solution)/shard_map/ppermute | solution.py:11
  219.6 74.8 %reduce-scatter.2.cloned.1.call-done = f32[1296,384]{1,0:T(8,128)} async-done(((f32[10368,384]{1,0:T(8,128)}), f32[1296,384]{1,0:T(8,128)}) %reduce-scatter.2.cloned.1.call-update) | async-done | bytes 1990672 | tf_op jit(solution)/shard_map/reduce_scatter | solution.py:101
  294.4 133.7 %all-reduce.14.cloned.1.call-done = f32[432,384]{1,0:T(8,128)} async-done(((f32[432,384]{1,0:T(8,128)}), f32[432,384]{1,0:T(8,128)}) %all-reduce.14.cloned.1.call-update) | async-done | bytes 663568 | tf_op jit(solution)/shard_map/psum | solution.py:99
  428.1 86.2 %all-reduce.16.cloned.1.call-done = f32[1296,384]{1,0:T(8,128)} async-done(((f32[1296,384]{1,0:T(8,128)}), f32[1296,384]{1,0:T(8,128)}) %all-reduce.16.cloned.1.call-update) | async-done | bytes 1990672 | tf_op jit(solution)/shard_map/psum | solution.py:100
  514.3 3.0 copy.65
  (165 shorter events, 107.4 us)
Async XLA Ops:
  7.2 11.3 %copy-start = (bf16[432,384]{1,0:T(8,128)(2,1)S(1)}, bf16[432,384]{1,0:T(8,128)(2,1)}, u32[]{:S(2)}) copy-start(bf16[432,384]{1,0:T(8,128)(2,1)} %param.8) | copy-start | bytes 995332
  7.2 58.1 %all-gather.2.cloned.1.call-start = ((), (), s32[]{:S(2)}) async-start(), calls=%async_computation.1 | async-start | bytes 8957952 | tf_op jit(solution)/shard_map/all_gather | solution.py:66
  7.9 286.4 %reduce-scatter.2.cloned.1.call-start = ((), (), s32[]{:S(2)}) async-start(), calls=%async_computation.3 | async-start | bytes 17915904 | tf_op jit(solution)/shard_map/reduce_scatter | solution.py:101
  9.7 6.6 %collective-permute-start = (bf16[256,16]{0,1:T(8,128)(2,1)S(1)}, bf16[256,16]{0,1:T(8,128)(2,1)S(1)}, u32[]{:S(2)}, u32[]{:S(2)}) collective-permute-start(bf16[256,16]{0,1:T(8,128)(2,1)S(1)} %slice.384), channel_id=1, source_target_pairs={{0,1},{1,2},{2,3},{4,5},{5,6},{6,7},{8,9},{9,10},{10,11},{12,13},{... | collective-permute-start | bytes 24584 | tf_op jit(solution)/shard_map/ppermute | solution.py:11
  18.5 2.0 copy-start.13
  20.5 7.4 %collective-permute-start.1 = (bf16[256,384]{1,0:T(8,128)(2,1)S(1)}, bf16[256,384]{1,0:T(8,128)(2,1)S(1)}, u32[]{:S(2)}, u32[]{:S(2)}) collective-permute-start(bf16[256,384]{1,0:T(8,128)(2,1)S(1)} %slice.517), channel_id=1, source_target_pairs={{0,1},{1,2},{2,3},{4,5},{5,6},{6,7},{8,9},{9,10},{10,11},{12,13},{... | collective-permute-start | bytes 589832 | tf_op jit(solution)/shard_map/ppermute | solution.py:11
  30.2 43.8 %copy-start.9 = (bf16[1297,384]{1,0:T(8,128)(2,1)}, bf16[1297,384]{1,0:T(8,128)(2,1)S(1)}, u32[]{:S(2)}) copy-start(bf16[1297,384]{1,0:T(8,128)(2,1)S(1)} %concatenate.47) | copy-start | bytes 2988292
  65.3 8.7 %copy-start.2 = (bf16[10368,384]{1,0:T(8,128)(2,1)S(1)}, bf16[10368,384]{1,0:T(8,128)(2,1)}, u32[]{:S(2)}) copy-start(bf16[10368,384]{1,0:T(8,128)(2,1)} %all-gather.2.cloned.1.call-done) | copy-start | bytes 23887876
  135.3 3.1 copy-start.10
  135.3 3.1 copy-start.11
  181.3 2.1 copy-start.7
  181.3 246.8 %all-reduce.14.cloned.1.call-start = ((), (), s32[]{:S(2)}) async-start(), calls=%async_computation.2 | async-start | bytes 1327104 | tf_op jit(solution)/shard_map/psum | solution.py:99
  183.4 1.9 copy-start.6
  183.4 5.7 %slice-start = ((s8[7962624]{0:T(1024)(128)(4,1)}), s8[4194304]{0:T(1024)(128)(4,1)S(1)}, s32[]{:S(2)}) async-start(s8[7962624]{0:T(1024)(128)(4,1)} %bitcast.44), calls=%async_computation.5 | async-start | bytes 8388608
  185.4 1.9 copy-start.5
  185.4 3.8 slice-start.1
  187.3 1.9 copy-start.4
  192.8 1.3 copy-start.8
  208.5 9.2 %copy-start.14 = (bf16[1024,432]{0,1:T(8,128)(2,1)S(1)}, bf16[1024,432]{0,1:T(8,128)(2,1)}, u32[]{:S(2)}) copy-start(bf16[1024,432]{0,1:T(8,128)(2,1)} %copy-done.13) | copy-start | bytes 2654212
  208.5 9.2 %copy-start.15 = (f32[1024,384]{1,0:T(8,128)S(1)}, f32[1024,384]{1,0:T(8,128)}, u32[]{:S(2)}) copy-start(f32[1024,384]{1,0:T(8,128)} %get-tuple-element.12) | copy-start | bytes 4718596
  208.5 9.2 %collective-permute-start.2 = (bf16[256,384]{1,0:T(8,128)(2,1)S(1)}, bf16[256,384]{1,0:T(8,128)(2,1)S(1)}, u32[]{:S(2)}, u32[]{:S(2)}) collective-permute-start(bf16[256,384]{1,0:T(8,128)(2,1)S(1)} %slice.1014), channel_id=1, source_target_pairs={{1,0},{2,1},{3,2},{5,4},{6,5},{7,6},{9,8},{10,9},{11,10},{13,12},{... | collective-permute-start | bytes 589832 | tf_op jit(solution)/shard_map/ppermute | solution.py:11
  219.5 294.8 %all-reduce.16.cloned.1.call-start = ((), (), s32[]{:S(2)}) async-start(), calls=%async_computation.4 | async-start | bytes 3981312 | tf_op jit(solution)/shard_map/psum | solution.py:100
  428.1 89.2 %copy-start.12 = (f32[432,384]{1,0:T(8,128)S(1)}, f32[432,384]{1,0:T(8,128)}, u32[]{:S(2)}) copy-start(f32[432,384]{1,0:T(8,128)} %all-reduce.14.cloned.1.call-done) | copy-start | bytes 1990660
  514.3 3.9 copy-start.1
  (1 other events, 1.3 us)
Sparse Core Ops, SparseCore 0:
  9.9 55.3 all-gather.1
  181.4 112.8 reduce-scatter.1
  301.0 127.0 all-reduce.13
  430.4 83.9 all-reduce.15
where the time goes:
time: 528 us; the launch traced here: 525 us
  waiting for transfers between devices  342 us (65%)
  matrix products  145 us (27%)
  between operations  15.4 us (3%)
  starting transfers between devices  10.6 us (2%)
  local copies, waits for them, and re-layouts  10 us (2%)
    psum x1, waiting for transfers between devices, shards(): grad_in = lax.psum(cross_dot(patch_in, dz_first), ('clip', 'tm'))  134 us
    psum x1, waiting for transfers between devices, shards(): summed = lax.psum(local_mid, 'tm')  86.2 us
    reduce_scatter x1, waiting for transfers between devices, shards(): grad_mid = lax.psum_scatter(summed, 'clip', scatter_dimension=0, tiled=True)  74.8 us
    dot_general x27, matrix products, shards(): jnp.dot(act_taps[k], w_full[k * chans:(k + 1) * chans], preferred_element...  70 us
    dot_general x28, matrix products, cross_dot(): lax.dot_general(left, right, (((0,), (0,)), ((), ())), preferred_element_...  47.7 us
    all_gather x1, waiting for transfers between devices, shards(): w_full = lax.all_gather(w_mid, 'clip', axis=0, tiled=True)  35.1 us
    dot_general x27, matrix products, shards(): lax.dot_general(piece, w_full[k * chans:(k + 1) * chans], (((1,), (1,)),...  25.7 us
    ppermute x3, waiting for transfers between devices, passed_along(): return lax.ppermute(block, axis, route)  11 us
  transfers between devices with their start and end apart: 7, of which 6 were waited for; matrix products, arithmetic and copies ran while one was open for 7% of the time, Pallas kernels for 0%

commit v1 on v0

--- a/solution.py
+++ b/solution.py
@@ -63,7 +63,12 @@
     act_prev = passed_along(act[count - 2 * plane :], "tm", 1)
     act_ext = jnp.concatenate([act_prev, act], axis=0)
     act_taps = tap_slices(act_ext, count, rows, cols, masks)
-    w_full = lax.all_gather(w_mid, "clip", axis=0, tiled=True)
+    ring = [w_mid]
+    for hop in range(7):
+        ring.append(lax.ppermute(ring[-1], "clip", [(dev, (dev + 1) % 8) for dev in range(8)]))
+    w_full = jnp.roll(
+        jnp.concatenate(ring[::-1], axis=0), (lax.axis_index("clip") + 1) * ring[0].shape[0], axis=0
+    )
     output = jnp.zeros((count, chans), jnp.float32)
     for k in range(27):
         output = output + jnp.dot(

time: 528 us -> 574 us (1.087)
  matrix products: 145 us -> 217 us
  waiting for transfers between devices: 342 us -> 303 us
  local copies, waits for them, and re-layouts: 10 us -> 20.2 us
    ppermute x0 -> x7, waiting for transfers between devices: none -> 80.5 us  [shards(): lax.ppermute(ring[-1], 'clip', [(dev, (dev + 1) % 8) for dev in range(8)])]
    dot_general x27, matrix products: 25.7 us -> 98.3 us  [shards(): lax.dot_general(piece, w_full[k * chans:(k + 1) * chans], (((1,), (1,)),...]
    reduce_scatter x1, waiting for transfers between devices: 74.8 us -> 4.47 us  [shards(): grad_mid = lax.psum_scatter(summed, 'clip', scatter_dimension=0, tiled=True)]
    all_gather x1 -> x0, waiting for transfers between devices: 35.1 us -> none  [shards(): w_full = lax.all_gather(w_mid, 'clip', axis=0, tiled=True)]
    psum x1, waiting for transfers between devices: 134 us -> 122 us  [shards(): grad_in = lax.psum(cross_dot(patch_in, dz_first), ('clip', 'tm'))]
    unnamed x39 -> x70, local copies, waits for them, and re-layouts: 4.89 us -> 14.5 us
  transfers between devices with their start and end apart: 7 -> 13, of which waited for: 6 -> 12; matrix products, arithmetic and copies ran while one was open for 7% -> 19% of each run, Pallas kernels for 0% -> 0%
where the time goes in v1:
time: 574 us; the launch traced here: 569 us
  waiting for transfers between devices  303 us (53%)
  matrix products  217 us (38%)
  local copies, waits for them, and re-layouts  20.2 us (4%)
  between operations  17 us (3%)
  starting transfers between devices  10.9 us (2%)
    psum x1, waiting for transfers between devices, shards(): grad_in = lax.psum(cross_dot(patch_in, dz_first), ('clip', 'tm'))  122 us
    dot_general x27, matrix products, shards(): lax.dot_general(piece, w_full[k * chans:(k + 1) * chans], (((1,), (1,)),...  98.3 us
    psum x1, waiting for transfers between devices, shards(): summed = lax.psum(local_mid, 'tm')  86 us
    ppermute x7, waiting for transfers between devices, shards(): lax.ppermute(ring[-1], 'clip', [(dev, (dev + 1) % 8) for dev in range(8)])  80.5 us
    dot_general x27, matrix products, shards(): jnp.dot(act_taps[k], w_full[k * chans:(k + 1) * chans], preferred_element...  68.6 us
    dot_general x28, matrix products, cross_dot(): lax.dot_general(left, right, (((0,), (0,)), ((), ())), preferred_element_...  47.7 us
    unnamed x70, local copies, waits for them, and re-layouts  14.5 us
  transfers between devices with their start and end apart: 13, of which 12 were waited for; matrix products, arithmetic and copies ran while one was open for 19% of the time, Pallas kernels for 0%

profile of v1, /device:TPU:0, one launch (start us, length us, event | category | flops | bytes accessed | tf_op | source)
XLA Modules:
  0.0 569.4 jit_solution(10820786007773092242)
XLA Ops:
  10.3 4.5 collective-permute-start
  16.5 7.0 %collective-permute-done.2 = bf16[1296,384]{1,0:T(8,128)(2,1)S(1)} collective-permute-done((bf16[1296,384]{1,0:T(8,128)(2,1)}, bf16[1296,384]{1,0:T(8,128)(2,1)S(1)}, u32[]{:S(2)}, u32[]{:S(2)}) %collective-permute-start.2) | collective-permute-done | bytes 995360 | tf_op jit(solution)/shard_map/ppermute | solution.py:68
  23.9 14.3 %collective-permute-done.3 = bf16[1296,384]{1,0:T(8,128)(2,1)S(1)} collective-permute-done((bf16[1296,384]{1,0:T(8,128)(2,1)S(1)}, bf16[1296,384]{1,0:T(8,128)(2,1)S(1)}, u32[]{:S(2)}, u32[]{:S(2)}) %collective-permute-start.3) | collective-permute-done | bytes 995360 | tf_op jit(solution)/shard_map/ppermute | solution.py:68
  38.6 14.1 %collective-permute-done.4 = bf16[1296,384]{1,0:T(8,128)(2,1)S(1)} collective-permute-done((bf16[1296,384]{1,0:T(8,128)(2,1)S(1)}, bf16[1296,384]{1,0:T(8,128)(2,1)S(1)}, u32[]{:S(2)}, u32[]{:S(2)}) %collective-permute-start.4) | collective-permute-done | bytes 995360 | tf_op jit(solution)/shard_map/ppermute | solution.py:68
  53.1 14.2 %collective-permute-done.5 = bf16[1296,384]{1,0:T(8,128)(2,1)S(1)} collective-permute-done((bf16[1296,384]{1,0:T(8,128)(2,1)S(1)}, bf16[1296,384]{1,0:T(8,128)(2,1)S(1)}, u32[]{:S(2)}, u32[]{:S(2)}) %collective-permute-start.5) | collective-permute-done | bytes 995360 | tf_op jit(solution)/shard_map/ppermute | solution.py:68
  67.7 14.1 %collective-permute-done.6 = bf16[1296,384]{1,0:T(8,128)(2,1)S(1)} collective-permute-done((bf16[1296,384]{1,0:T(8,128)(2,1)S(1)}, bf16[1296,384]{1,0:T(8,128)(2,1)S(1)}, u32[]{:S(2)}, u32[]{:S(2)}) %collective-permute-start.6) | collective-permute-done | bytes 995360 | tf_op jit(solution)/shard_map/ppermute | solution.py:68
  82.2 14.3 %collective-permute-done.7 = bf16[1296,384]{1,0:T(8,128)(2,1)} collective-permute-done((bf16[1296,384]{1,0:T(8,128)(2,1)S(1)}, bf16[1296,384]{1,0:T(8,128)(2,1)}, u32[]{:S(2)}, u32[]{:S(2)}) %collective-permute-start.7) | collective-permute-done | bytes 995360 | tf_op jit(solution)/shard_map/ppermute | solution.py:68
  98.7 4.2 collective-permute-start.1
  103.0 3.1 collective-permute-done.1
  171.9 17.9 %broadcast_multiply_fusion.8 = (bf16[1024,384]{1,0:T(8,128)(2,1)}, bf16[1024,384]{1,0:T(8,128)(2,1)}, bf16[1024,384]{1,0:T(8,128)(2,1)}, bf16[1024,384]{1,0:T(8,...) fusion(bf16[1024]{0:T(1024)(128)(2,1)S(1)} %and_convert_fusion., ...), kind=kOutput, calls=%fused_computation.214 | convolution fusion | flops 318898176 | bytes 50647044 | tf_op jit(solution)/shard_map/dot_general | solution.py:74
  189.8 3.1 convolution_dynamic-update-slice_fusion.26
  240.0 3.1 fusion.53
  246.1 3.1 fusion.50
  249.2 3.1 fusion.48
  252.3 3.2 fusion.47
  258.6 3.2 fusion.44
  283.0 3.3 fusion.32
  292.3 3.1 fusion.52
  301.6 3.1 fusion.43
  316.9 18.4 %fusion.24 = f32[1280,384]{1,0:T(8,128)S(1)} fusion(f32[1280,384]{1,0:T(8,128)} %fusion.54, f32[1280,384]{1,0:T(8,128)} %fusion.51, f32[1280,384]{1,0:T(8,128)} %fusion.48, f32[1280,384]{1,0:T(8,128)} %fusion.45, f32[1280,384]{1,0:T(8,128)} %fusion.42, f32[1280,384]{1,0:T(8,128)} %fusion.39, f32[1280,384]{1,0:T(8,128)} %fusion.36, f32[1280,384]{1,0:T(8,128)} %fusion.33, ...), kind=kOutput, calls=%fused_computation.42 | convolution fusion | flops 390266880 | bytes 54165508 | tf_op jit(solution)/shard_map/dot_general | solution.py:92
  337.0 6.6 %collective-permute-done.9 = bf16[256,384]{1,0:T(8,128)(2,1)S(1)} collective-permute-done((bf16[256,384]{1,0:T(8,128)(2,1)S(1)}, bf16[256,384]{1,0:T(8,128)(2,1)S(1)}, u32[]{:S(2)}, u32[]{:S(2)}) %collective-permute-start.9) | collective-permute-done | bytes 196640 | tf_op jit(solution)/shard_map/ppermute | solution.py:11
  345.5 4.5 reduce-scatter.2.cloned.1.call-done
  349.9 121.9 %all-reduce.14.cloned.1.call-done = f32[432,384]{1,0:T(8,128)} async-done(((f32[432,384]{1,0:T(8,128)}), f32[432,384]{1,0:T(8,128)}) %all-reduce.14.cloned.1.call-update) | async-done | bytes 663568 | tf_op jit(solution)/shard_map/psum | solution.py:104
  471.9 86.0 %all-reduce.16.cloned.1.call-done = f32[1296,384]{1,0:T(8,128)} async-done(((f32[1296,384]{1,0:T(8,128)}), f32[1296,384]{1,0:T(8,128)}) %all-reduce.16.cloned.1.call-update) | async-done | bytes 1990672 | tf_op jit(solution)/shard_map/psum | solution.py:105
  (206 shorter events, 179.1 us)
Async XLA Ops:
  8.0 88.7 %copy-start = (bf16[432,384]{1,0:T(8,128)(2,1)S(1)}, bf16[432,384]{1,0:T(8,128)(2,1)}, u32[]{:S(2)}) copy-start(bf16[432,384]{1,0:T(8,128)(2,1)} %param.8) | copy-start | bytes 995332
  8.0 341.9 %reduce-scatter.2.cloned.1.call-start = ((), (), s32[]{:S(2)}) async-start(), calls=%async_computation.2 | async-start | bytes 17915904 | tf_op jit(solution)/shard_map/reduce_scatter | solution.py:106
  8.1 15.5 %collective-permute-start.2 = (bf16[1296,384]{1,0:T(8,128)(2,1)}, bf16[1296,384]{1,0:T(8,128)(2,1)S(1)}, u32[]{:S(2)}, u32[]{:S(2)}) collective-permute-start(bf16[1296,384]{1,0:T(8,128)(2,1)} %param.9), channel_id=1, source_target_pairs={{0,4},{4,8},{8,12},{12,16},{16,20},{20,24},{24,28},{28,0},{1,5},{5... | collective-permute-start | bytes 2985992 | tf_op jit(solution)/shard_map/ppermute | solution.py:68
  10.3 6.1 %collective-permute-start = (bf16[256,16]{0,1:T(8,128)(2,1)S(1)}, bf16[256,16]{0,1:T(8,128)(2,1)S(1)}, u32[]{:S(2)}, u32[]{:S(2)}) collective-permute-start(bf16[256,16]{0,1:T(8,128)(2,1)S(1)} %slice.384), channel_id=1, source_target_pairs={{0,1},{1,2},{2,3},{4,5},{5,6},{6,7},{8,9},{9,10},{10,11},{12,13},{... | collective-permute-start | bytes 24584 | tf_op jit(solution)/shard_map/ppermute | solution.py:11
  23.6 14.6 %collective-permute-start.3 = (bf16[1296,384]{1,0:T(8,128)(2,1)S(1)}, bf16[1296,384]{1,0:T(8,128)(2,1)S(1)}, u32[]{:S(2)}, u32[]{:S(2)}) collective-permute-start(bf16[1296,384]{1,0:T(8,128)(2,1)S(1)} %collective-permute-done.2), channel_id=1, source_target_pairs={{0,4},{4,8},{8,12},{12,16},{16,20},{20,24},{24,28},{28,0},{1,5},{5... | collective-permute-start | bytes 2985992 | tf_op jit(solution)/shard_map/ppermute | solution.py:68
  38.1 58.4 %copy-start.13 = (bf16[1296,384]{1,0:T(8,128)(2,1)}, bf16[1296,384]{1,0:T(8,128)(2,1)S(1)}, u32[]{:S(2)}) copy-start(bf16[1296,384]{1,0:T(8,128)(2,1)S(1)} %collective-permute-done.3) | copy-start | bytes 2985988
  38.1 14.6 %collective-permute-start.4 = (bf16[1296,384]{1,0:T(8,128)(2,1)S(1)}, bf16[1296,384]{1,0:T(8,128)(2,1)S(1)}, u32[]{:S(2)}, u32[]{:S(2)}) collective-permute-start(bf16[1296,384]{1,0:T(8,128)(2,1)S(1)} %collective-permute-done.3), channel_id=1, source_target_pairs={{0,4},{4,8},{8,12},{12,16},{16,20},{20,24},{24,28},{28,0},{1,5},{5... | collective-permute-start | bytes 2985992 | tf_op jit(solution)/shard_map/ppermute | solution.py:68
  52.7 43.9 %copy-start.15 = (bf16[1296,384]{1,0:T(8,128)(2,1)}, bf16[1296,384]{1,0:T(8,128)(2,1)S(1)}, u32[]{:S(2)}) copy-start(bf16[1296,384]{1,0:T(8,128)(2,1)S(1)} %collective-permute-done.4) | copy-start | bytes 2985988
  52.7 14.6 %collective-permute-start.5 = (bf16[1296,384]{1,0:T(8,128)(2,1)S(1)}, bf16[1296,384]{1,0:T(8,128)(2,1)S(1)}, u32[]{:S(2)}, u32[]{:S(2)}) collective-permute-start(bf16[1296,384]{1,0:T(8,128)(2,1)S(1)} %collective-permute-done.4), channel_id=1, source_target_pairs={{0,4},{4,8},{8,12},{12,16},{16,20},{20,24},{24,28},{28,0},{1,5},{5... | collective-permute-start | bytes 2985992 | tf_op jit(solution)/shard_map/ppermute | solution.py:68
  67.2 29.3 %copy-start.17 = (bf16[1296,384]{1,0:T(8,128)(2,1)}, bf16[1296,384]{1,0:T(8,128)(2,1)S(1)}, u32[]{:S(2)}) copy-start(bf16[1296,384]{1,0:T(8,128)(2,1)S(1)} %collective-permute-done.5) | copy-start | bytes 2985988
  67.2 14.6 %collective-permute-start.6 = (bf16[1296,384]{1,0:T(8,128)(2,1)S(1)}, bf16[1296,384]{1,0:T(8,128)(2,1)S(1)}, u32[]{:S(2)}, u32[]{:S(2)}) collective-permute-start(bf16[1296,384]{1,0:T(8,128)(2,1)S(1)} %collective-permute-done.5), channel_id=1, source_target_pairs={{0,4},{4,8},{8,12},{12,16},{16,20},{20,24},{24,28},{28,0},{1,5},{5... | collective-permute-start | bytes 2985992 | tf_op jit(solution)/shard_map/ppermute | solution.py:68
  81.8 14.8 %copy-start.19 = (bf16[1296,384]{1,0:T(8,128)(2,1)}, bf16[1296,384]{1,0:T(8,128)(2,1)S(1)}, u32[]{:S(2)}) copy-start(bf16[1296,384]{1,0:T(8,128)(2,1)S(1)} %collective-permute-done.6) | copy-start | bytes 2985988
  81.8 14.7 %collective-permute-start.7 = (bf16[1296,384]{1,0:T(8,128)(2,1)S(1)}, bf16[1296,384]{1,0:T(8,128)(2,1)}, u32[]{:S(2)}, u32[]{:S(2)}) collective-permute-start(bf16[1296,384]{1,0:T(8,128)(2,1)S(1)} %collective-permute-done.6), channel_id=1, source_target_pairs={{0,4},{4,8},{8,12},{12,16},{16,20},{20,24},{24,28},{28,0},{1,5},{5... | collective-permute-start | bytes 2985992 | tf_op jit(solution)/shard_map/ppermute | solution.py:68
  96.5 14.9 %collective-permute-start.8 = (bf16[1296,384]{1,0:T(8,128)(2,1)}, bf16[1296,384]{1,0:T(8,128)(2,1)}, u32[]{:S(2)}, u32[]{:S(2)}) collective-permute-start(bf16[1296,384]{1,0:T(8,128)(2,1)} %collective-permute-done.7), channel_id=1, source_target_pairs={{0,4},{4,8},{8,12},{12,16},{16,20},{20,24},{24,28},{28,0},{1,5},{5... | collective-permute-start | bytes 2985992 | tf_op jit(solution)/shard_map/ppermute | solution.py:68
  98.7 7.4 %collective-permute-start.1 = (bf16[256,384]{1,0:T(8,128)(2,1)S(1)}, bf16[256,384]{1,0:T(8,128)(2,1)S(1)}, u32[]{:S(2)}, u32[]{:S(2)}) collective-permute-start(bf16[256,384]{1,0:T(8,128)(2,1)S(1)} %slice.517), channel_id=1, source_target_pairs={{0,1},{1,2},{2,3},{4,5},{5,6},{6,7},{8,9},{9,10},{10,11},{12,13},{... | collective-permute-start | bytes 589832 | tf_op jit(solution)/shard_map/ppermute | solution.py:11
  108.8 26.9 %copy-start.9 = (bf16[1297,384]{1,0:T(8,128)(2,1)}, bf16[1297,384]{1,0:T(8,128)(2,1)S(1)}, u32[]{:S(2)}) copy-start(bf16[1297,384]{1,0:T(8,128)(2,1)S(1)} %concatenate.53) | copy-start | bytes 2988292
  108.8 5.3 copy-start.20
  121.2 48.9 %copy-start.11 = (bf16[20736,384]{1,0:T(8,128)(2,1)}, bf16[20736,384]{1,0:T(8,128)(2,1)S(1)}, u32[]{:S(2)}) copy-start(bf16[20736,384]{1,0:T(8,128)(2,1)S(1)} %constant_dynamic-update-slice_fusion.29) | copy-start | bytes 47775748
  235.8 236.0 %all-reduce.14.cloned.1.call-start = ((), (), s32[]{:S(2)}) async-start(), calls=%async_computation.1 | async-start | bytes 1327104 | tf_op jit(solution)/shard_map/psum | solution.py:104
  335.3 8.3 %copy-start.24 = (bf16[1024,432]{0,1:T(8,128)(2,1)S(1)}, bf16[1024,432]{0,1:T(8,128)(2,1)}, u32[]{:S(2)}) copy-start(bf16[1024,432]{0,1:T(8,128)(2,1)} %copy-done.23) | copy-start | bytes 2654212
  335.3 8.3 %copy-start.25 = (f32[1024,384]{1,0:T(8,128)S(1)}, f32[1024,384]{1,0:T(8,128)}, u32[]{:S(2)}) copy-start(f32[1024,384]{1,0:T(8,128)} %get-tuple-element.12) | copy-start | bytes 4718596
  335.3 8.2 %collective-permute-start.9 = (bf16[256,384]{1,0:T(8,128)(2,1)S(1)}, bf16[256,384]{1,0:T(8,128)(2,1)S(1)}, u32[]{:S(2)}, u32[]{:S(2)}) collective-permute-start(bf16[256,384]{1,0:T(8,128)(2,1)S(1)} %slice.881), channel_id=1, source_target_pairs={{1,0},{2,1},{3,2},{5,4},{6,5},{7,6},{9,8},{10,9},{11,10},{13,12},{... | collective-permute-start | bytes 589832 | tf_op jit(solution)/shard_map/ppermute | solution.py:11
  345.4 212.5 %all-reduce.16.cloned.1.call-start = ((), (), s32[]{:S(2)}) async-start(), calls=%async_computation.3 | async-start | bytes 3981312 | tf_op jit(solution)/shard_map/psum | solution.py:105
  471.9 89.0 %copy-start.22 = (f32[432,384]{1,0:T(8,128)S(1)}, f32[432,384]{1,0:T(8,128)}, u32[]{:S(2)}) copy-start(f32[432,384]{1,0:T(8,128)} %all-reduce.14.cloned.1.call-done) | copy-start | bytes 1990660
  (15 other events, 37.7 us)
Sparse Core Ops, SparseCore 0:
  236.0 113.9 reduce-scatter.1
Sparse Core Ops, SparseCore 1:
  345.5 126.3 all-reduce.13
  474.1 83.7 all-reduce.15
